TPU v7x, 32 devices: a whole 2x2x4 slice. The times are simulated.
32 devices in a mesh: dp: 4 (over z), tensor: 4 (over y, x), section: 2 (over core).
Axes of the slice: x: 2, y: 2, z: 4, core: 2. Of those that a mesh axis runs over, the one named last changes fastest.
Arguments:
- grads: bfloat16 [4, 2, 768, 768], P('dp', 'section', 'tensor'), may hold values from -6 to 6
- errors: float32 [4, 2, 768, 768], P('dp', 'section', 'tensor'), may hold values from -3 to 3
- q_prev: float32 [2, 768, 32], P('section'), may hold values from -0.21875 to 0.21875
- p_root: float32 [2, 32, 32], P('section')
- q_root: float32 [2, 32, 32], P('section')
- momentum: float32 [2, 768, 768], P('section', 'tensor')
- weights: float32 [2, 768, 768], P('section', 'tensor'), may hold values from -0.21875 to 0.21875
- vec_grads: float32 [4, 2, 3, 768], P('dp', 'section', None, 'tensor'), may hold values from -6 to 6
- vec_momentum: float32 [2, 3, 768], P('section', None, 'tensor'), may hold values from -6 to 6
- vec_params: float32 [2, 3, 768], P('section', None, 'tensor'), may hold values from -3 to 3
Outputs:
- errors_out: float32 [4, 2, 768, 768], P('dp', 'section', 'tensor')
- p_factor: float32 [2, 768, 32], P('section', 'tensor')
- q_factor: float32 [2, 768, 32], P('section')
- momentum_out: float32 [2, 768, 768], P('section', 'tensor')
- weights_out: float32 [2, 768, 768], P('section', 'tensor')
- vec_momentum_out: float32 [2, 3, 768], P('section', None, 'tensor')
- vec_params_out: float32 [2, 3, 768], P('section', None, 'tensor')
All inputs are finite; a program needn't handle non-finite values.
Results may differ from a plain program's by a relative error of at most 0.0003.
Values sent between devices are 32-bit elements; how exact they have to be, the bound alone decides.
A program may use at most 64 MiB of HBM per device.

v0:
```python
import jax
import jax.numpy as jnp
from jax import lax
from jax.sharding import PartitionSpec as P

D = 768
HIGH = lax.Precision.HIGHEST


def shards(
    grads, errors, q_prev, p_root, q_root, momentum, weights, vec_grads, vec_momentum, vec_params
):
    replicas = lax.axis_size("dp")
    vec_local = vec_grads[0, 0]
    vec_sum = lax.psum(vec_local, "dp")
    merged = grads[0, 0].astype(jnp.float32) + errors[0, 0]
    p_local = jnp.dot(merged, q_prev[0], precision=HIGH, preferred_element_type=jnp.float32)
    p_sum = lax.psum(p_local, "dp")
    p_factor = jnp.dot(p_sum, p_root[0], precision=HIGH, preferred_element_type=jnp.float32)
    q_partial = lax.dot_general(
        merged,
        p_factor,
        (((0,), (0,)), ((), ())),
        precision=HIGH,
        preferred_element_type=jnp.float32,
    )
    q_whole = lax.psum(q_partial, ("dp", "tensor"))
    q_factor = jnp.dot(q_whole, q_root[0], precision=HIGH, preferred_element_type=jnp.float32)
    approx = (
        lax.dot_general(
            p_factor,
            q_factor,
            (((1,), (1,)), ((), ())),
            precision=HIGH,
            preferred_element_type=jnp.float32,
        )
        / replicas
    )
    errors_out = merged - approx
    vec_mean = vec_sum / replicas
    momentum_out = 0.9 * momentum[0] + approx
    vec_momentum_out = 0.9 * vec_momentum[0] + vec_mean
    local_total = jnp.sum(momentum_out * momentum_out) + jnp.sum(
        vec_momentum_out * vec_momentum_out
    )
    total = lax.psum(local_total, ("tensor", "section"))
    scale = 0.05 / jnp.sqrt(total / (2 * D * D + 6 * D) + 1e-06)
    weights_out = weights[0] - scale * momentum_out
    vec_params_out = vec_params[0] - scale * vec_momentum_out
    return (
        errors_out[None, None],
        p_factor[None],
        q_factor[None],
        momentum_out[None],
        weights_out[None],
        vec_momentum_out[None],
        vec_params_out[None],
    )


def solution(mesh):
    in_specs = (
        P("dp", "section", "tensor", None),
        P("dp", "section", "tensor", None),
        P("section", None, None),
        P("section", None, None),
        P("section", None, None),
        P("section", "tensor", None),
        P("section", "tensor", None),
        P("dp", "section", None, "tensor"),
        P("section", None, "tensor"),
        P("section", None, "tensor"),
    )
    out_specs = (
        P("dp", "section", "tensor", None),
        P("section", "tensor", None),
        P("section", None, None),
        P("section", "tensor", None),
        P("section", "tensor", None),
        P("section", None, "tensor"),
        P("section", None, "tensor"),
    )
    return jax.shard_map(shards, mesh=mesh, in_specs=in_specs, out_specs=out_specs, check_vma=False)
```

profile of v0, /device:TPU:0, one launch (start us, length us, event | category | flops | bytes accessed | tf_op | source)
XLA Modules:
  0.0 168.7 jit_solution(3444834635649647149)
XLA Ops:
  7.2 0.0 copy-start
  7.2 0.0 all-reduce.3.cloned.1.call-start
  7.2 0.7 copy.26
  7.9 0.2 copy-done
  8.1 0.0 copy-start.1
  8.1 0.0 copy-start.2
  8.1 1.8 %fusion.3 = f32[192,32]{1,0:T(8,128)S(1)} fusion(f32[1,1,192,768]{3,2,1,0:T(8,128)} %param.11, bf16[1,1,192,768]{3,2,1,0:T(8,128)(2,1)} %param.10, f32[1,768,32]{1,2,0:T(8,128)S(1)} %copy-done), kind=kOutput, calls=%fused_computation.7 | convolution fusion | flops 56918016 | bytes 1007616 | tf_op jit(solution)/shard_map/dot_general | solution.py:17
  9.9 0.0 copy-start.7
  9.9 22.7 %all-reduce = (f32[192,32]{1,0:T(8,128)S(1)}, f32[3,192]{1,0:T(4,128)S(1)}) all-reduce(f32[192,32]{1,0:T(8,128)S(1)} %fusion.3, f32[3,192]{1,0:T(4,128)S(1)} %bitcast.52), channel_id=1, replica_groups=mesh['dp'=4,'tensor'=4,'section'=2] {'dp'}, use_global_device_ids=true, to_apply=%region_0.0 | all-reduce | flops 6720 | bytes 53760 | tf_op jit(solution)/shard_map/psum | solution.py:18
  32.6 0.0 copy-done.7
  32.6 0.3 fusion.9
  32.9 0.0 copy-done.1
  32.9 0.0 copy-done.2
  32.9 0.0 copy-start.6
  32.9 0.0 copy-start.9
  33.0 0.0 copy-start.8
  33.0 2.2 %fusion.1 = f32[768,32]{1,0:T(8,128)} fusion(f32[192,32]{0,1:T(8,128)S(1)} %fusion.9, f32[1,1,192,768]{3,2,1,0:T(8,128)S(1)} %copy-done.1, bf16[1,1,192,768]{3,2,1,0:T(8,128)(2,1)S(1)} %copy-done.2), kind=kOutput, calls=%fused_computation.5 | convolution fusion | flops 56918016 | bytes 1007616 | tf_op jit(solution)/shard_map/dot_general | solution.py:20
  35.2 0.0 copy-start.3
  35.2 0.0 all-reduce.3.cloned.1.call-update
  35.2 0.0 copy-done.9
  35.2 0.6 multiply_reduce_fusion.1
  35.8 105.7 %all-reduce.3.cloned.1.call-done = f32[768,32]{1,0:T(8,128)} async-done(((f32[768,32]{1,0:T(8,128)}), f32[768,32]{1,0:T(8,128)}) %all-reduce.3.cloned.1.call-update) | async-done | bytes 98320 | tf_op jit(solution)/shard_map/psum | solution.py:27
  141.5 0.0 copy-done.8
  141.5 1.5 fusion.7
  143.1 0.0 copy-done.6
  143.1 0.0 copy-done.3
  143.1 0.0 copy-start.5
  143.1 0.0 copy-start.4
  143.1 1.4 multiply_reduce_fusion
  144.5 0.0 copy-done.5
  145.8 0.6 broadcast_in_dim.26
  146.4 12.3 %psum.31 = f32[]{:T(128)} all-reduce(f32[]{:T(128)S(6)} %add.31), channel_id=1, replica_groups=mesh['dp'=4,'tensor'=4,'section'=2] {'tensor','section'}, use_global_device_ids=true, to_apply=%region_5.0 | all-reduce | flops 1 | bytes 8 | tf_op jit(solution)/shard_map/psum | solution.py:46
  159.3 0.0 copy-start.10
  159.3 0.6 copy-done.10
  160.0 0.6 broadcast_in_dim.27
  160.6 0.0 copy-done.4
  160.6 1.3 fusion
  (1 shorter events, 0.0 us)
Async XLA Ops:
  7.2 0.9 copy-start
  7.2 134.4 %all-reduce.3.cloned.1.call-start = ((), (), s32[]{:S(2)}) async-start(), calls=%async_computation | async-start | bytes 786432 | tf_op jit(solution)/shard_map/psum | solution.py:27
  8.1 24.8 %copy-start.1 = (f32[1,1,192,768]{3,2,1,0:T(8,128)S(1)}, f32[1,1,192,768]{3,2,1,0:T(8,128)}, u32[]{:S(2)}) copy-start(f32[1,1,192,768]{3,2,1,0:T(8,128)} %param.11) | copy-start | bytes 1769476
  8.1 24.9 %copy-start.2 = (bf16[1,1,192,768]{3,2,1,0:T(8,128)(2,1)S(1)}, bf16[1,1,192,768]{3,2,1,0:T(8,128)(2,1)}, u32[]{:S(2)}) copy-start(bf16[1,1,192,768]{3,2,1,0:T(8,128)(2,1)} %param.10) | copy-start | bytes 884740
  9.9 22.7 %copy-start.7 = (f32[1,32,32]{2,1,0:T(8,128)S(1)}, f32[1,32,32]{2,1,0:T(8,128)}, u32[]{:S(2)}) copy-start(f32[1,32,32]{2,1,0:T(8,128)} %param.13) | copy-start | bytes 12292
  32.9 110.1 %copy-start.6 = (f32[192,32]{0,1:T(8,128)}, f32[192,32]{0,1:T(8,128)S(1)}, u32[]{:S(2)}) copy-start(f32[192,32]{0,1:T(8,128)S(1)} %fusion.9) | copy-start | bytes 73732
  32.9 2.3 %copy-start.9 = (f32[1,3,192]{2,0,1:T(1,128)S(1)}, f32[1,3,192]{2,0,1:T(1,128)}, u32[]{:S(2)}) copy-start(f32[1,3,192]{2,0,1:T(1,128)} %param.18) | copy-start | bytes 6916
  33.0 108.6 %copy-start.8 = (f32[1,32,32]{2,1,0:T(8,128)S(1)}, f32[1,32,32]{2,1,0:T(8,128)}, u32[]{:S(2)}) copy-start(f32[1,32,32]{2,1,0:T(8,128)} %param.14) | copy-start | bytes 12292
  35.2 107.9 %copy-start.3 = (f32[1,192,768]{2,1,0:T(8,128)S(1)}, f32[1,192,768]{2,1,0:T(8,128)}, u32[]{:S(2)}) copy-start(f32[1,192,768]{2,1,0:T(8,128)} %param.15) | copy-start | bytes 1769476
  143.1 1.4 copy-start.5
  143.1 17.5 %copy-start.4 = (f32[1,192,768]{2,1,0:T(8,128)S(1)}, f32[1,192,768]{2,1,0:T(8,128)}, u32[]{:S(2)}) copy-start(f32[1,192,768]{2,1,0:T(8,128)} %param.16) | copy-start | bytes 1769476
  159.3 0.7 copy-start.10
Sparse Core Ops, SparseCore 0:
  35.3 106.1 all-reduce.2
where the time goes:
time: 169 us
  waiting for transfers between devices  106 us (63%)
  blocking collectives  35 us (21%)
  between operations  16.2 us (10%)
  matrix products  7.21 us (4%)
  local copies, waits for them, and re-layouts  2.7 us (2%)
  other arithmetic  1.89 us (1%)
    psum x1, waiting for transfers between devices, shards(): q_whole = lax.psum(q_partial, ('dp', 'tensor'))  106 us
    psum x1, blocking collectives, shards(): p_sum = lax.psum(p_local, 'dp')  22.7 us
    psum x1, blocking collectives, shards(): total = lax.psum(local_total, ('tensor', 'section'))  12.3 us
  transfers between devices with their start and end apart: 1, of which 1 were waited for; matrix products, arithmetic and copies ran while one was open for 0% of the time, Pallas kernels for 0%

commit v1 on v0

--- a/solution.py
+++ b/solution.py
@@ -5,6 +5,7 @@
 
 D = 768
 HIGH = lax.Precision.HIGHEST
+recover_slots = lambda buf: lax.all_gather(buf, ("dp", "tensor")).sum(axis=0)
 
 
 def shards(
@@ -24,7 +25,7 @@
         precision=HIGH,
         preferred_element_type=jnp.float32,
     )
-    q_whole = lax.psum(q_partial, ("dp", "tensor"))
+    q_whole = recover_slots(q_partial)
     q_factor = jnp.dot(q_whole, q_root[0], precision=HIGH, preferred_element_type=jnp.float32)
     approx = (
         lax.dot_general(

time: 169 us -> 120 us (0.71)
  waiting for transfers between devices: 106 us -> 55.8 us
  local copies, waits for them, and re-layouts: 2.7 us -> 4.4 us
    psum x1 -> x0, waiting for transfers between devices: 106 us -> none  [shards(): q_whole = lax.psum(q_partial, ('dp', 'tensor'))]
    all_gather x0 -> x1, waiting for transfers between devices: none -> 55.8 us  [lax.all_gather(buf, ('dp', 'tensor')).sum(axis=0)]
    unnamed x23 -> x22, local copies, waits for them, and re-layouts: 1.53 us -> 3.24 us
  transfers between devices with their start and end apart: 1 -> 1, of which waited for: 1 -> 1; matrix products, arithmetic and copies ran while one was open for 0% -> 1% of each run, Pallas kernels for 0% -> 0%
where the time goes in v1:
time: 120 us
  waiting for transfers between devices  55.8 us (46%)
  blocking collectives  35 us (29%)
  between operations  16.2 us (14%)
  matrix products  6.47 us (5%)
  local copies, waits for them, and re-layouts  4.4 us (4%)
  other arithmetic  2.13 us (2%)
    all_gather x1, waiting for transfers between devices, lax.all_gather(buf, ('dp', 'tensor')).sum(axis=0)  55.8 us
    psum x1, blocking collectives, shards(): p_sum = lax.psum(p_local, 'dp')  22.7 us
    psum x1, blocking collectives, shards(): total = lax.psum(local_total, ('tensor', 'section'))  12.3 us
    unnamed x22, local copies, waits for them, and re-layouts  3.24 us
  transfers between devices with their start and end apart: 1, of which 1 were waited for; matrix products, arithmetic and copies ran while one was open for 1% of the time, Pallas kernels for 0%

profile of v1, /device:TPU:0, one launch (start us, length us, event | category | flops | bytes accessed | tf_op | source)
XLA Modules:
  0.0 119.9 jit_solution(13537530717081118306)
XLA Ops:
  7.2 0.0 copy-start
  7.2 0.0 copy-start.1
  7.2 0.0 copy-start.8
  7.2 0.0 all-gather.3.cloned.1.call-start
  7.2 0.7 copy.28
  8.0 0.1 copy-done
  8.1 1.7 %fusion.3 = f32[192,32]{1,0:T(8,128)S(1)} fusion(f32[1,1,192,768]{3,2,1,0:T(8,128)} %param.11, bf16[1,1,192,768]{3,2,1,0:T(8,128)(2,1)} %param.10, f32[1,768,32]{1,2,0:T(8,128)S(1)} %copy-done), kind=kOutput, calls=%fused_computation.8 | convolution fusion | flops 56918016 | bytes 1007616 | tf_op jit(solution)/shard_map/dot_general | solution.py:18
  9.8 22.7 %all-reduce = (f32[192,32]{1,0:T(8,128)S(1)}, f32[3,192]{1,0:T(4,128)S(1)}) all-reduce(f32[192,32]{1,0:T(8,128)S(1)} %fusion.3, f32[3,192]{1,0:T(4,128)S(1)} %bitcast.58), channel_id=1, replica_groups=mesh['dp'=4,'tensor'=4,'section'=2] {'dp'}, use_global_device_ids=true, to_apply=%region_0.0 | all-reduce | flops 6720 | bytes 53760 | tf_op jit(solution)/shard_map/psum | solution.py:19
  32.5 1.0 fusion.9
  33.5 0.0 copy-done.1
  33.5 0.0 copy-start.6
  33.5 2.1 %fusion.1 = f32[768,32]{0,1:T(8,128)} fusion(f32[192,32]{0,1:T(8,128)S(1)} %fusion.9, f32[1,1,192,768]{3,2,1,0:T(8,128)S(1)} %copy-done.1, bf16[1,1,192,768]{3,2,1,0:T(8,128)(2,1)} %param.10), kind=kOutput, calls=%fused_computation.6 | convolution fusion | flops 56918016 | bytes 1007616 | tf_op jit(solution)/shard_map/dot_general | solution.py:21
  35.6 0.0 all-gather.3.cloned.1.call-update
  35.6 0.0 copy-done.8
  35.7 0.6 multiply_reduce_fusion.1
  36.3 55.8 %all-gather.3.cloned.1.call-done = f32[12288,32]{0,1:T(8,128)} async-done(((f32[768,32]{0,1:T(8,128)}), f32[12288,32]{0,1:T(8,128)}) %all-gather.3.cloned.1.call-update) | async-done | bytes 1572880 | tf_op jit(solution)/shard_map/all_gather | solution.py:8
  92.0 1.9 %copy.21 = f32[4,8,16,768]{3,2,1,0:T(8,128)S(1)} copy(f32[4,8,16,768]{3,1,2,0:T(8,128)} %bitcast.55) | data formatting | bytes 3145728
  93.9 0.0 copy-start.7
  93.9 0.0 copy-start.3
  93.9 0.0 copy-start.9
  93.9 0.0 copy-start.2
  94.0 0.0 copy-start.4
  94.0 0.2 bitcast_reduce_fusion
  94.2 0.4 copy-done.7
  94.6 0.3 fusion.7
  94.9 0.0 copy-done.6
  94.9 0.1 copy-done.3
  95.0 0.0 copy-start.5
  95.0 1.4 %multiply_reduce_fusion = (f32[]{:T(128)}, f32[192,768]{1,0:T(8,128)S(1)}) fusion(f32[1,192,768]{2,1,0:T(8,128)S(1)} %copy-done.3, f32[192,32]{0,1:T(8,128)S(1)} %fusion.9, f32[768,32]{0,1:T(8,128)S(1)} %fusion.7), kind=kOutput, calls=%fused_computation.11 | convolution fusion | flops 57360384 | bytes 1302532 | tf_op jit(solution)/shard_map/dot_general | solution.py:31
  97.6 0.6 broadcast_in_dim.26
  98.2 12.3 %psum.23 = f32[]{:T(128)} all-reduce(f32[]{:T(128)S(6)} %add.29), channel_id=1, replica_groups=mesh['dp'=4,'tensor'=4,'section'=2] {'tensor','section'}, use_global_device_ids=true, to_apply=%region_5.0 | all-reduce | flops 1 | bytes 8 | tf_op jit(solution)/shard_map/psum | solution.py:47
  111.2 0.0 copy-done.9
  111.2 0.6 broadcast_in_dim.27
  111.8 0.0 copy-done.2
  111.8 0.0 copy-done.4
  111.8 1.3 %fusion = (f32[1,192,768]{2,1,0:T(8,128)}, f32[1,192,768]{2,1,0:T(8,128)}, f32[1,1,192,768]{3,2,1,0:T(8,128)}) fusion(f32[1,192,768]{2,1,0:T(8,128)S(1)} %copy-done.4, f32[]{:T(128)S(6)} %div.23, f32[192,768]{1,0:T(8,128)S(1)} %get-tuple-element.15, f32[1,192,768]{2,1,0:T(8,128)S(1)} %copy-done.3, f32[1,1,192,768]{3,2,1,0:T(8,128)S(1)} %copy-done.1, ...), kind=kLoop, calls=%fused_computation.3 | loop fusion | flops 1032192 | bytes 4423684 | tf_op jit(solution)/shard_map/broadcast_in_dim | solution.py:56
  113.1 0.0 copy-done.5
  (1 shorter events, 0.0 us)
Async XLA Ops:
  7.2 0.9 copy-start
  7.2 26.3 %copy-start.1 = (f32[1,1,192,768]{3,2,1,0:T(8,128)S(1)}, f32[1,1,192,768]{3,2,1,0:T(8,128)}, u32[]{:S(2)}) copy-start(f32[1,1,192,768]{3,2,1,0:T(8,128)} %param.11) | copy-start | bytes 1769476
  7.2 28.5 %copy-start.8 = (f32[1,3,192]{2,0,1:T(1,128)S(1)}, f32[1,3,192]{2,0,1:T(1,128)}, u32[]{:S(2)}) copy-start(f32[1,3,192]{2,0,1:T(1,128)} %param.18) | copy-start | bytes 6916
  7.2 84.8 %all-gather.3.cloned.1.call-start = ((), (), s32[]{:S(2)}) async-start(), calls=%async_computation | async-start | bytes 1671168 | tf_op jit(solution)/shard_map/all_gather | solution.py:8
  33.5 61.4 %copy-start.6 = (f32[192,32]{0,1:T(8,128)}, f32[192,32]{0,1:T(8,128)S(1)}, u32[]{:S(2)}) copy-start(f32[192,32]{0,1:T(8,128)S(1)} %fusion.9) | copy-start | bytes 73732
  93.9 0.7 copy-start.7
  93.9 1.1 copy-start.3
  93.9 17.3 %copy-start.9 = (f32[1,3,192]{2,0,1:T(1,128)S(1)}, f32[1,3,192]{2,0,1:T(1,128)}, u32[]{:S(2)}) copy-start(f32[1,3,192]{2,0,1:T(1,128)} %param.19) | copy-start | bytes 6916
  93.9 17.9 %copy-start.2 = (bf16[1,1,192,768]{3,2,1,0:T(8,128)(2,1)S(1)}, bf16[1,1,192,768]{3,2,1,0:T(8,128)(2,1)}, u32[]{:S(2)}) copy-start(bf16[1,1,192,768]{3,2,1,0:T(8,128)(2,1)} %param.10) | copy-start | bytes 884740
  94.0 17.9 %copy-start.4 = (f32[1,192,768]{2,1,0:T(8,128)S(1)}, f32[1,192,768]{2,1,0:T(8,128)}, u32[]{:S(2)}) copy-start(f32[1,192,768]{2,1,0:T(8,128)} %param.16) | copy-start | bytes 1769476
  95.0 18.1 %copy-start.5 = (f32[768,32]{0,1:T(8,128)}, f32[768,32]{0,1:T(8,128)S(1)}, u32[]{:S(2)}) copy-start(f32[768,32]{0,1:T(8,128)S(1)} %fusion.7) | copy-start | bytes 294916
Sparse Core Ops, SparseCore 0:
  35.8 56.2 all-gather.2

commit v2 on v0

--- a/solution.py
+++ b/solution.py
@@ -24,7 +24,9 @@
         precision=HIGH,
         preferred_element_type=jnp.float32,
     )
-    q_whole = lax.psum(q_partial, ("dp", "tensor"))
+    q_whole = q_partial
+    for mesh_axis in ("tensor", "dp"):
+        q_whole = lax.psum(q_whole, mesh_axis)
     q_factor = jnp.dot(q_whole, q_root[0], precision=HIGH, preferred_element_type=jnp.float32)
     approx = (
         lax.dot_general(

time: 169 us -> 145 us (0.86)
  waiting for transfers between devices: 106 us -> 80.8 us
    psum x1 -> x2, waiting for transfers between devices: 106 us -> 80.8 us  [shards(): q_whole = lax.psum(q_whole, mesh_axis)]
  transfers between devices with their start and end apart: 1 -> 2, of which waited for: 1 -> 2; matrix products, arithmetic and copies ran while one was open for 0% -> 0% of each run, Pallas kernels for 0% -> 0%
where the time goes in v2:
time: 145 us
  waiting for transfers between devices  80.8 us (56%)
  blocking collectives  35.1 us (24%)
  between operations  16.2 us (11%)
  matrix products  7.21 us (5%)
  local copies, waits for them, and re-layouts  3.35 us (2%)
  other arithmetic  1.89 us (1%)
    psum x2, waiting for transfers between devices, shards(): q_whole = lax.psum(q_whole, mesh_axis)  80.8 us
    psum x1, blocking collectives, shards(): p_sum = lax.psum(p_local, 'dp')  22.7 us
    psum x1, blocking collectives, shards(): total = lax.psum(local_total, ('tensor', 'section'))  12.4 us
  transfers between devices with their start and end apart: 2, of which 2 were waited for; matrix products, arithmetic and copies ran while one was open for 0% of the time, Pallas kernels for 0%

profile of v2, /device:TPU:0, one launch (start us, length us, event | category | flops | bytes accessed | tf_op | source)
XLA Modules:
  0.0 144.6 jit_solution(6738236280038735940)
XLA Ops:
  7.2 0.0 copy-start
  7.2 0.0 all-reduce.4.cloned.1.call-start
  7.2 0.7 copy.26
  7.9 0.2 copy-done
  8.1 0.0 copy-start.1
  8.1 0.0 copy-start.2
  8.1 1.8 %fusion.3 = f32[192,32]{1,0:T(8,128)S(1)} fusion(f32[1,1,192,768]{3,2,1,0:T(8,128)} %param.11, bf16[1,1,192,768]{3,2,1,0:T(8,128)(2,1)} %param.10, f32[1,768,32]{1,2,0:T(8,128)S(1)} %copy-done), kind=kOutput, calls=%fused_computation.7 | convolution fusion | flops 56918016 | bytes 1007616 | tf_op jit(solution)/shard_map/dot_general | solution.py:17
  9.9 0.0 copy-start.7
  9.9 22.7 %all-reduce = (f32[192,32]{1,0:T(8,128)S(1)}, f32[3,192]{1,0:T(4,128)S(1)}) all-reduce(f32[192,32]{1,0:T(8,128)S(1)} %fusion.3, f32[3,192]{1,0:T(4,128)S(1)} %bitcast.52), channel_id=1, replica_groups=mesh['dp'=4,'tensor'=4,'section'=2] {'dp'}, use_global_device_ids=true, to_apply=%region_0.0 | all-reduce | flops 6720 | bytes 53760 | tf_op jit(solution)/shard_map/psum | solution.py:18
  32.6 0.0 copy-done.7
  32.6 0.3 fusion.9
  32.9 0.0 copy-done.1
  32.9 0.0 copy-done.2
  32.9 0.0 copy-start.6
  32.9 2.2 %fusion.1 = f32[768,32]{1,0:T(8,128)} fusion(f32[192,32]{0,1:T(8,128)S(1)} %fusion.9, f32[1,1,192,768]{3,2,1,0:T(8,128)S(1)} %copy-done.1, bf16[1,1,192,768]{3,2,1,0:T(8,128)(2,1)S(1)} %copy-done.2), kind=kOutput, calls=%fused_computation.5 | convolution fusion | flops 56918016 | bytes 1007616 | tf_op jit(solution)/shard_map/dot_general | solution.py:20
  35.1 0.0 copy-start.3
  35.1 0.0 all-reduce.4.cloned.1.call-update
  35.2 0.0 all-reduce.6.cloned.1.call-start
  35.2 42.5 %all-reduce.4.cloned.1.call-done = f32[768,32]{1,0:T(8,128)} async-done(((f32[768,32]{1,0:T(8,128)}), f32[768,32]{1,0:T(8,128)}) %all-reduce.4.cloned.1.call-update) | async-done | bytes 98320 | tf_op jit(solution)/shard_map/psum | solution.py:29
  77.7 0.0 copy-start.9
  77.7 0.0 copy-start.8
  77.7 0.0 all-reduce.6.cloned.1.call-update
  77.8 0.7 copy-done.9
  78.4 0.6 multiply_reduce_fusion.1
  79.0 38.3 %all-reduce.6.cloned.1.call-done = f32[768,32]{1,0:T(8,128)} async-done(((f32[768,32]{1,0:T(8,128)}), f32[768,32]{1,0:T(8,128)}) %all-reduce.6.cloned.1.call-update) | async-done | bytes 98320 | tf_op jit(solution)/shard_map/psum | solution.py:29
  117.3 0.0 copy-done.8
  117.3 1.5 %fusion.7 = f32[768,32]{0,1:T(8,128)S(1)} fusion(f32[768,32]{1,0:T(8,128)} %all-reduce.6.cloned.1.call-done, f32[1,32,32]{2,1,0:T(8,128)S(1)} %copy-done.8), kind=kOutput, calls=%fused_computation.13 | convolution fusion | flops 9437184 | bytes 200704 | tf_op jit(solution)/shard_map/dot_general | solution.py:30
  118.8 0.0 copy-done.6
  118.8 0.0 copy-done.3
  118.9 0.0 copy-start.5
  118.9 0.0 copy-start.4
  118.9 1.4 multiply_reduce_fusion
  120.2 0.0 copy-done.5
  121.5 0.6 broadcast_in_dim.26
  122.1 12.4 %psum.39 = f32[]{:T(128)} all-reduce(f32[]{:T(128)S(6)} %add.33), channel_id=1, replica_groups=mesh['dp'=4,'tensor'=4,'section'=2] {'tensor','section'}, use_global_device_ids=true, to_apply=%region_6.0 | all-reduce | flops 1 | bytes 8 | tf_op jit(solution)/shard_map/psum | solution.py:48
  135.2 0.0 copy-start.10
  135.2 0.6 copy-done.10
  135.9 0.6 broadcast_in_dim.27
  136.4 0.0 copy-done.4
  136.4 1.3 fusion
  (1 shorter events, 0.0 us)
Async XLA Ops:
  7.2 0.9 copy-start
  7.2 70.6 %all-reduce.4.cloned.1.call-start = ((), (), s32[]{:S(2)}) async-start(), calls=%async_computation | async-start | bytes 786432 | tf_op jit(solution)/shard_map/psum | solution.py:29
  8.1 24.8 %copy-start.1 = (f32[1,1,192,768]{3,2,1,0:T(8,128)S(1)}, f32[1,1,192,768]{3,2,1,0:T(8,128)}, u32[]{:S(2)}) copy-start(f32[1,1,192,768]{3,2,1,0:T(8,128)} %param.11) | copy-start | bytes 1769476
  8.1 24.9 %copy-start.2 = (bf16[1,1,192,768]{3,2,1,0:T(8,128)(2,1)S(1)}, bf16[1,1,192,768]{3,2,1,0:T(8,128)(2,1)}, u32[]{:S(2)}) copy-start(bf16[1,1,192,768]{3,2,1,0:T(8,128)(2,1)} %param.10) | copy-start | bytes 884740
  9.9 22.7 %copy-start.7 = (f32[1,32,32]{2,1,0:T(8,128)S(1)}, f32[1,32,32]{2,1,0:T(8,128)}, u32[]{:S(2)}) copy-start(f32[1,32,32]{2,1,0:T(8,128)} %param.13) | copy-start | bytes 12292
  32.9 85.9 %copy-start.6 = (f32[192,32]{0,1:T(8,128)}, f32[192,32]{0,1:T(8,128)S(1)}, u32[]{:S(2)}) copy-start(f32[192,32]{0,1:T(8,128)S(1)} %fusion.9) | copy-start | bytes 73732
  35.1 83.7 %copy-start.3 = (f32[1,192,768]{2,1,0:T(8,128)S(1)}, f32[1,192,768]{2,1,0:T(8,128)}, u32[]{:S(2)}) copy-start(f32[1,192,768]{2,1,0:T(8,128)} %param.15) | copy-start | bytes 1769476
  35.2 82.1 %all-reduce.6.cloned.1.call-start = ((), (), s32[]{:S(2)}) async-start(), calls=%async_computation.1 | async-start | bytes 786432 | tf_op jit(solution)/shard_map/psum | solution.py:29
  77.7 0.7 copy-start.9
  77.7 39.6 %copy-start.8 = (f32[1,32,32]{2,1,0:T(8,128)S(1)}, f32[1,32,32]{2,1,0:T(8,128)}, u32[]{:S(2)}) copy-start(f32[1,32,32]{2,1,0:T(8,128)} %param.14) | copy-start | bytes 12292
  118.9 1.4 copy-start.5
  118.9 17.6 %copy-start.4 = (f32[1,192,768]{2,1,0:T(8,128)S(1)}, f32[1,192,768]{2,1,0:T(8,128)}, u32[]{:S(2)}) copy-start(f32[1,192,768]{2,1,0:T(8,128)} %param.16) | copy-start | bytes 1769476
  135.2 0.7 copy-start.10
Sparse Core Ops, SparseCore 0:
  35.3 42.4 all-reduce.3
  80.2 37.0 all-reduce.5
